TPU v7x, 32 devices: a whole 2x2x4 slice. The times are simulated.
32 devices in a mesh: section: 2 (over core), seq: 4 (over y, x), tensor: 4 (over z).
Axes of the slice: x: 2, y: 2, z: 4, core: 2. Of those that a mesh axis runs over, the one named last changes fastest.
Arguments:
- tokens: bfloat16 [4096, 1024], P('seq', 'tensor'), may hold values from -6 to 6
- segments: int32 [8, 512], P('seq'), may hold values from 0 to 3, never falling along the last dimension, each value on 1 to 256 neighbouring positions
- cotangent: bfloat16 [4096, 1024], P('seq', 'tensor'), may hold values from -6 to 6
- norm1_gain: bfloat16 [2, 1024], P('section', ('tensor', 'seq')), may hold values from 0.5 to 1.5
- norm1_bias: bfloat16 [2, 1024], P('section', ('tensor', 'seq')), may hold values from -3 to 3
- qkv_weight: bfloat16 [2, 1024, 16, 192], P('section', 'seq', 'tensor'), may hold values from -0.1875 to 0.1875
- qv_bias: bfloat16 [2, 16, 128], P('section', 'tensor', 'seq'), may hold values from -4 to 4
- out_weight: bfloat16 [2, 16, 64, 1024], P('section', 'tensor', None, 'seq'), may hold values from -0.75 to 0.75
- out_bias: bfloat16 [2, 1024], P('section', ('tensor', 'seq')), may hold values from -3 to 3
- norm2_gain: bfloat16 [2, 1024], P('section', ('tensor', 'seq')), may hold values from 0.5 to 1.5
- norm2_bias: bfloat16 [2, 1024], P('section', ('tensor', 'seq')), may hold values from -3 to 3
- up_weight: bfloat16 [2, 1024, 4096], P('section', 'seq', 'tensor'), may hold values from -0.1875 to 0.1875
- up_bias: bfloat16 [2, 4096], P('section', ('tensor', 'seq')), may hold values from -4 to 4
- down_weight: bfloat16 [2, 4096, 1024], P('section', 'tensor', 'seq'), may hold values from -0.09375 to 0.09375
- down_bias: bfloat16 [2, 1024], P('section', ('tensor', 'seq')), may hold values from -3 to 3
Outputs:
- section_out: bfloat16 [2, 4096, 1024], P('section', 'seq', 'tensor')
- input_grad: bfloat16 [2, 4096, 1024], P('section', 'seq', 'tensor')
- grad_norm1_gain: float32 [2, 1024], P('section', ('tensor', 'seq'))
- grad_norm1_bias: float32 [2, 1024], P('section', ('tensor', 'seq'))
- grad_qkv_weight: float32 [2, 1024, 16, 192], P('section', 'seq', 'tensor')
- grad_qv_bias: float32 [2, 16, 128], P('section', 'tensor', 'seq')
- grad_out_weight: float32 [2, 16, 64, 1024], P('section', 'tensor', None, 'seq')
- grad_out_bias: float32 [2, 1024], P('section', ('tensor', 'seq'))
- grad_norm2_gain: float32 [2, 1024], P('section', ('tensor', 'seq'))
- grad_norm2_bias: float32 [2, 1024], P('section', ('tensor', 'seq'))
- grad_up_weight: float32 [2, 1024, 4096], P('section', 'seq', 'tensor')
- grad_up_bias: float32 [2, 4096], P('section', ('tensor', 'seq'))
- grad_down_weight: float32 [2, 4096, 1024], P('section', 'tensor', 'seq')
- grad_down_bias: float32 [2, 1024], P('section', ('tensor', 'seq'))
Inputs may be any that keep to these rules, and one draw needn't show every extreme that they name: `segments`: along each sequence the document numbers never fall; every document holds 1 to 256 positions.
All inputs are finite; a program needn't handle non-finite values.
Results may differ from a plain program's by a relative error of at most 0.02.
Values may be sent and summed in bfloat16 or wider, within the bound.
A program may use at most 192 MiB of HBM per device.

v0:
```python
import math

import jax
import jax.numpy as jnp
from jax import lax
from jax.sharding import PartitionSpec as P

D = 1024
MB = 2


epsilon = 1e-05
floor_value = -1e30


def passed_along(shard, axis, by):
    devices = lax.axis_size(axis)
    pairs = [(i, i + by) for i in range(devices) if 0 <= i + by < devices]
    return lax.ppermute(shard, axis, pairs)


def row_totals(first, second):
    return lax.psum((jnp.sum(first, axis=1), jnp.sum(second, axis=1)), "tensor")


def norm_forward(rows, gain, shift):
    total, square = row_totals(rows, rows * rows)
    average = total / D
    variance = square / D - average * average
    scale = lax.rsqrt(variance + epsilon)
    centred = (rows - average[:, None]) * scale[:, None]
    return (centred, scale, centred * gain + shift)


def norm_backward(grad, centred, scale, gain):
    scaled = grad * gain
    total, along = row_totals(scaled, scaled * centred)
    return scale[:, None] * (scaled - total[:, None] / D - centred * along[:, None] / D)


def full_rows(piece):
    return lax.all_gather(piece, "tensor", axis=1, tiled=True)


def head_sums(partial_rows):
    return lax.psum_scatter(
        partial_rows.astype(jnp.bfloat16), "tensor", scatter_dimension=1, tiled=True
    ).astype(jnp.float32)


def grad_full(piece):
    return lax.all_gather(piece, "tensor", axis=1, tiled=True)


def back_sums(partial_rows):
    return lax.psum_scatter(
        partial_rows.astype(jnp.bfloat16), "tensor", scatter_dimension=1, tiled=True
    ).astype(jnp.float32)


def allowed_mask(segment):
    length = segment.shape[1]
    place = lax.broadcasted_iota(jnp.int32, (length, length), 0)
    other = lax.broadcasted_iota(jnp.int32, (length, length), 1)
    same = segment[:, :, None] == segment[:, None, :]
    return (same & (other <= place)[None])[:, None]


def attention_scores(query, keys, segment):
    head_dim = query.shape[-1]
    factor = 1.0 / math.sqrt(head_dim)
    scores = jnp.einsum("sqhe,skhe->shqk", query, keys, preferred_element_type=jnp.float32) * factor
    return (jnp.where(allowed_mask(segment), scores, floor_value), factor)


def forward(rows, segment, weights):
    gain1, bias1, w_qkv, b_qv, w_out, b_out, gain2, bias2, w_up, b_up, w_down, b_down = weights
    count_rows = rows.shape[0]
    heads = w_qkv.shape[1]
    head_dim = w_qkv.shape[2] // 3
    shape4 = (segment.shape[0], segment.shape[1], heads, head_dim)
    centred1, scale1, normed1 = norm_forward(rows, gain1, bias1)
    normed_whole = full_rows(normed1.astype(jnp.bfloat16))
    mixed = jnp.einsum("rd,dhe->rhe", normed_whole, w_qkv, preferred_element_type=jnp.float32)
    query = (mixed[..., :head_dim] + b_qv[:, :head_dim]).astype(jnp.bfloat16).reshape(shape4)
    keys = mixed[..., head_dim : 2 * head_dim].astype(jnp.bfloat16).reshape(shape4)
    values = (mixed[..., 2 * head_dim :] + b_qv[:, head_dim:]).astype(jnp.bfloat16).reshape(shape4)
    masked, factor = attention_scores(query, keys, segment)
    highest_score = jnp.max(masked, axis=-1, keepdims=True)
    raised = jnp.exp(masked - highest_score)
    total = jnp.sum(raised, axis=-1, keepdims=True)
    chance = (raised / total).astype(jnp.bfloat16)
    logsum = highest_score + jnp.log(total)
    context = jnp.einsum("shqk,skhe->sqhe", chance, values, preferred_element_type=jnp.float32)
    context = context.reshape(count_rows, heads * head_dim).astype(jnp.bfloat16)
    attn_part = jnp.dot(
        context, w_out.reshape(heads * head_dim, w_out.shape[2]), preferred_element_type=jnp.float32
    )
    hidden = rows + (head_sums(attn_part) + b_out)
    centred2, scale2, normed2 = norm_forward(hidden, gain2, bias2)
    normed2_whole = full_rows(normed2.astype(jnp.bfloat16))
    upper = jnp.dot(normed2_whole, w_up, preferred_element_type=jnp.float32) + b_up
    active = jax.nn.gelu(upper, approximate=True).astype(jnp.bfloat16)
    branch = head_sums(jnp.dot(active, w_down, preferred_element_type=jnp.float32)) + b_down
    output = (hidden + branch).astype(jnp.bfloat16)
    kept = (
        centred1,
        scale1,
        normed_whole,
        query,
        keys,
        values,
        logsum,
        context,
        centred2,
        scale2,
        normed2_whole,
        upper,
        active,
    )
    return (output, kept)


def gelu_value(upper):
    return jax.nn.gelu(upper, approximate=True)


def backward(grad_out, segment, weights, kept):
    gain1, bias1, w_qkv, b_qv, w_out, b_out, gain2, bias2, w_up, b_up, w_down, b_down = weights
    (
        centred1,
        scale1,
        normed_whole,
        query,
        keys,
        values,
        logsum,
        context,
        centred2,
        scale2,
        normed2_whole,
        upper,
        active,
    ) = kept
    count_rows = grad_out.shape[0]
    heads = w_qkv.shape[1]
    head_dim = w_qkv.shape[2] // 3
    shape4 = query.shape
    grad_branch = grad_out.astype(jnp.bfloat16)
    branch_whole = grad_full(grad_branch)
    grad_down = jnp.einsum("rf,rd->fd", active, branch_whole, preferred_element_type=jnp.float32)
    grad_active = jnp.einsum("rd,fd->rf", branch_whole, w_down, preferred_element_type=jnp.float32)
    grad_upper = jax.vjp(gelu_value, upper)[1](grad_active)[0].astype(jnp.bfloat16)
    grad_up = jnp.einsum("rd,rf->df", normed2_whole, grad_upper, preferred_element_type=jnp.float32)
    grad_normed2 = back_sums(
        jnp.einsum("rf,df->rd", grad_upper, w_up, preferred_element_type=jnp.float32)
    )
    grad_hidden = grad_out + norm_backward(grad_normed2, centred2, scale2, gain2)
    grad_attn = grad_hidden.astype(jnp.bfloat16)
    attn_whole = grad_full(grad_attn)
    out_matrix = w_out.reshape(heads * head_dim, w_out.shape[2])
    grad_out_w = jnp.einsum("rc,rd->cd", context, attn_whole, preferred_element_type=jnp.float32)
    grad_context = jnp.einsum(
        "rd,cd->rc", attn_whole, out_matrix, preferred_element_type=jnp.float32
    )
    grad_context = grad_context.astype(jnp.bfloat16).reshape(shape4)
    masked, factor = attention_scores(query, keys, segment)
    chance_full = jnp.exp(masked - logsum)
    chance = chance_full.astype(jnp.bfloat16)
    grad_chance = jnp.einsum(
        "sqhe,skhe->shqk", grad_context, values, preferred_element_type=jnp.float32
    )
    delta = jnp.sum(grad_chance * chance_full, axis=-1, keepdims=True)
    grad_scores = (chance_full * (grad_chance - delta)).astype(jnp.bfloat16)
    grad_query = (
        jnp.einsum("shqk,skhe->sqhe", grad_scores, keys, preferred_element_type=jnp.float32)
        * factor
    ).astype(jnp.bfloat16)
    grad_keys = (
        jnp.einsum("shqk,sqhe->skhe", grad_scores, query, preferred_element_type=jnp.float32)
        * factor
    ).astype(jnp.bfloat16)
    grad_values = jnp.einsum(
        "shqk,sqhe->skhe", chance, grad_context, preferred_element_type=jnp.float32
    ).astype(jnp.bfloat16)
    grad_mixed = jnp.concatenate([grad_query, grad_keys, grad_values], axis=-1).reshape(
        count_rows, heads, 3 * head_dim
    )
    grad_qkv = jnp.einsum(
        "rd,rhe->dhe", normed_whole, grad_mixed, preferred_element_type=jnp.float32
    )
    grad_qv = jnp.concatenate(
        [
            jnp.sum(grad_query.astype(jnp.float32), axis=(0, 1)),
            jnp.sum(grad_values.astype(jnp.float32), axis=(0, 1)),
        ],
        axis=-1,
    )
    grad_normed1 = back_sums(
        jnp.einsum("rhe,dhe->rd", grad_mixed, w_qkv, preferred_element_type=jnp.float32)
    )
    grad_rows_total = grad_hidden + norm_backward(grad_normed1, centred1, scale1, gain1)
    grads = (
        jnp.sum(grad_normed1 * centred1, axis=0),
        jnp.sum(grad_normed1, axis=0),
        grad_qkv,
        grad_qv,
        grad_out_w.reshape(w_out.shape),
        jnp.sum(grad_attn.astype(jnp.float32), axis=0),
        jnp.sum(grad_normed2 * centred2, axis=0),
        jnp.sum(grad_normed2, axis=0),
        grad_up,
        jnp.sum(grad_upper.astype(jnp.float32), axis=0),
        grad_down,
        jnp.sum(grad_branch.astype(jnp.float32), axis=0),
    )
    return (grad_rows_total.astype(jnp.bfloat16), grads)


def body(
    tokens,
    segments,
    cotangent,
    norm1_gain,
    norm1_bias,
    qkv_weight,
    qv_bias,
    out_weight,
    out_bias,
    norm2_gain,
    norm2_bias,
    up_weight,
    up_bias,
    down_weight,
    down_bias,
):
    section = lax.axis_index("section")
    first_section = section == 0
    gathered = (
        lax.all_gather(norm1_gain[0], "seq", axis=0, tiled=True),
        lax.all_gather(norm1_bias[0], "seq", axis=0, tiled=True),
        lax.all_gather(qkv_weight[0], "seq", axis=0, tiled=True),
        lax.all_gather(qv_bias[0], "seq", axis=1, tiled=True),
        lax.all_gather(out_weight[0], "seq", axis=2, tiled=True),
        lax.all_gather(out_bias[0], "seq", axis=0, tiled=True),
        lax.all_gather(norm2_gain[0], "seq", axis=0, tiled=True),
        lax.all_gather(norm2_bias[0], "seq", axis=0, tiled=True),
        lax.all_gather(up_weight[0], "seq", axis=0, tiled=True),
        lax.all_gather(up_bias[0], "seq", axis=0, tiled=True),
        lax.all_gather(down_weight[0], "seq", axis=1, tiled=True),
        lax.all_gather(down_bias[0], "seq", axis=0, tiled=True),
    )
    weights = (
        gathered[0].astype(jnp.float32),
        gathered[1].astype(jnp.float32),
        gathered[2],
        gathered[3].astype(jnp.float32),
        gathered[4],
        gathered[5].astype(jnp.float32),
        gathered[6].astype(jnp.float32),
        gathered[7].astype(jnp.float32),
        gathered[8],
        gathered[9].astype(jnp.float32),
        gathered[10],
        gathered[11].astype(jnp.float32),
    )
    rows_batch = tokens.shape[0] // MB
    seqs_batch = segments.shape[0] // MB
    width_local = tokens.shape[1]
    received = jnp.zeros((rows_batch, width_local), jnp.bfloat16)
    outputs = jnp.zeros(tokens.shape, jnp.bfloat16)
    stash = []
    for tick in range(MB + 1):
        own = min(tick, MB - 1)
        batch = tick - section
        valid = (batch >= 0) & (batch < MB)
        placed = jnp.clip(batch, 0, MB - 1)
        entry = jnp.where(
            first_section, tokens[own * rows_batch : (own + 1) * rows_batch], received
        )
        segment = lax.dynamic_slice_in_dim(segments, placed * seqs_batch, seqs_batch, 0)
        result, kept = forward(entry.astype(jnp.float32), segment, weights)
        stash.append((entry, segment))
        current = lax.dynamic_slice_in_dim(outputs, placed * rows_batch, rows_batch, 0)
        outputs = lax.dynamic_update_slice_in_dim(
            outputs, jnp.where(valid, result, current), placed * rows_batch, 0
        )
        if tick < MB:
            received = passed_along(result, "section", 1)
    totals = jax.tree.map(lambda item: jnp.zeros(item.shape, jnp.float32), gathered)
    returned = jnp.zeros((rows_batch, width_local), jnp.bfloat16)
    input_grads = jnp.zeros(tokens.shape, jnp.bfloat16)
    for tick in range(MB + 1):
        own = min(tick, MB - 1)
        batch = tick - (1 - section)
        valid = (batch >= 0) & (batch < MB)
        placed = jnp.clip(batch, 0, MB - 1)
        grad_in = jnp.where(
            first_section, returned, cotangent[own * rows_batch : (own + 1) * rows_batch]
        ).astype(jnp.float32)
        earlier = stash[max(tick - 1, 0)]
        later = stash[min(tick + 1, MB)]
        picked = jax.tree.map(
            lambda left, right: jnp.where(first_section, left, right), earlier, later
        )
        entry = picked[0]
        segment = picked[1]
        kept = forward(entry.astype(jnp.float32), segment, weights)[1]
        grad_rows_out, grads = backward(grad_in, segment, weights, kept)
        totals = jax.tree.map(lambda acc, new: acc + jnp.where(valid, new, 0.0), totals, grads)
        current = lax.dynamic_slice_in_dim(input_grads, placed * rows_batch, rows_batch, 0)
        input_grads = lax.dynamic_update_slice_in_dim(
            input_grads, jnp.where(valid, grad_rows_out, current), placed * rows_batch, 0
        )
        if tick < MB:
            returned = passed_along(grad_rows_out, "section", -1)
    reduced = (
        lax.psum_scatter(
            totals[0].astype(jnp.bfloat16), "seq", scatter_dimension=0, tiled=True
        ).astype(jnp.float32),
        lax.psum_scatter(
            totals[1].astype(jnp.bfloat16), "seq", scatter_dimension=0, tiled=True
        ).astype(jnp.float32),
        lax.psum_scatter(
            totals[2].astype(jnp.bfloat16), "seq", scatter_dimension=0, tiled=True
        ).astype(jnp.float32),
        lax.psum_scatter(
            totals[3].astype(jnp.bfloat16), "seq", scatter_dimension=1, tiled=True
        ).astype(jnp.float32),
        lax.psum_scatter(
            totals[4].astype(jnp.bfloat16), "seq", scatter_dimension=2, tiled=True
        ).astype(jnp.float32),
        lax.psum_scatter(
            totals[5].astype(jnp.bfloat16), "seq", scatter_dimension=0, tiled=True
        ).astype(jnp.float32),
        lax.psum_scatter(
            totals[6].astype(jnp.bfloat16), "seq", scatter_dimension=0, tiled=True
        ).astype(jnp.float32),
        lax.psum_scatter(
            totals[7].astype(jnp.bfloat16), "seq", scatter_dimension=0, tiled=True
        ).astype(jnp.float32),
        lax.psum_scatter(
            totals[8].astype(jnp.bfloat16), "seq", scatter_dimension=0, tiled=True
        ).astype(jnp.float32),
        lax.psum_scatter(
            totals[9].astype(jnp.bfloat16), "seq", scatter_dimension=0, tiled=True
        ).astype(jnp.float32),
        lax.psum_scatter(
            totals[10].astype(jnp.bfloat16), "seq", scatter_dimension=1, tiled=True
        ).astype(jnp.float32),
        lax.psum_scatter(
            totals[11].astype(jnp.bfloat16), "seq", scatter_dimension=0, tiled=True
        ).astype(jnp.float32),
    )
    return (outputs[None], input_grads[None]) + tuple((item[None] for item in reduced))


def solution(mesh):
    return jax.shard_map(
        body,
        mesh=mesh,
        in_specs=(
            P("seq", "tensor"),
            P("seq", None),
            P("seq", "tensor"),
            P("section", ("tensor", "seq")),
            P("section", ("tensor", "seq")),
            P("section", "seq", "tensor", None),
            P("section", "tensor", "seq"),
            P("section", "tensor", None, "seq"),
            P("section", ("tensor", "seq")),
            P("section", ("tensor", "seq")),
            P("section", ("tensor", "seq")),
            P("section", "seq", "tensor"),
            P("section", ("tensor", "seq")),
            P("section", "tensor", "seq"),
            P("section", ("tensor", "seq")),
        ),
        out_specs=(
            P("section", "seq", "tensor"),
            P("section", "seq", "tensor"),
            P("section", ("tensor", "seq")),
            P("section", ("tensor", "seq")),
            P("section", "seq", "tensor", None),
            P("section", "tensor", "seq"),
            P("section", "tensor", None, "seq"),
            P("section", ("tensor", "seq")),
            P("section", ("tensor", "seq")),
            P("section", ("tensor", "seq")),
            P("section", "seq", "tensor"),
            P("section", ("tensor", "seq")),
            P("section", "tensor", "seq"),
            P("section", ("tensor", "seq")),
        ),
        check_vma=False,
    )
```

profile of v0, /device:TPU:0, one launch (start us, length us, event | category | flops | bytes accessed | tf_op | source)
XLA Modules:
  0.0 1450.4 jit_solution(4128099430230138480)
XLA Ops:
  67.1 30.9 %all-gather.70.cloned.1.call-done = bf16[1,1024,4,192]{1,3,2,0:T(8,128)(2,1)} async-done(((bf16[1,256,4,192]{1,3,2,0:T(8,128)(2,1)}), bf16[1,1024,4,192]{1,3,2,0:T(8,128)(2,1)}) %all-gather.70.cloned.1.call-update) | async-done | bytes 1572880 | tf_op jit(solution)/shard_map/all_gather | solution.py:242
  109.8 26.2 %reduce-scatter.23.cloned.1.call-done = bf16[512,256]{1,0:T(8,128)(2,1)} async-done(((bf16[512,1024]{1,0:T(8,128)(2,1)}), bf16[512,256]{1,0:T(8,128)(2,1)}) %reduce-scatter.23.cloned.1.call-update) | async-done | bytes 262160 | tf_op jit(solution)/shard_map/reduce_scatter | solution.py:46
  171.2 36.9 %all-gather.72.cloned.1.call-done = bf16[1,1024,1024]{2,1,0:T(8,128)(2,1)} async-done(((bf16[1,256,1024]{2,1,0:T(8,128)(2,1)}), bf16[1,1024,1024]{2,1,0:T(8,128)(2,1)}) %all-gather.72.cloned.1.call-update) | async-done | bytes 2097168 | tf_op jit(solution)/shard_map/all_gather | solution.py:248
  208.1 31.9 %all-gather.36.cloned.1.call-done = bf16[512,1024]{1,0:T(8,128)(2,1)} async-done(((bf16[512,256]{1,0:T(8,128)(2,1)}), bf16[512,1024]{1,0:T(8,128)(2,1)}) %all-gather.36.cloned.1.call-update) | async-done | bytes 1048592 | tf_op jit(solution)/shard_map/all_gather | solution.py:42
  246.3 25.7 %reduce-scatter.25.cloned.1.call-done = bf16[512,256]{1,0:T(8,128)(2,1)} async-done(((bf16[512,1024]{1,0:T(8,128)(2,1)}), bf16[512,256]{1,0:T(8,128)(2,1)}) %reduce-scatter.25.cloned.1.call-update) | async-done | bytes 262160 | tf_op jit(solution)/shard_map/reduce_scatter | solution.py:46
  286.7 28.2 %all-gather.46.cloned.1.call-done = bf16[512,1024]{1,0:T(8,128)(2,1)} async-done(((bf16[512,256]{1,0:T(8,128)(2,1)}), bf16[512,1024]{1,0:T(8,128)(2,1)}) %all-gather.46.cloned.1.call-update) | async-done | bytes 1048592 | tf_op jit(solution)/shard_map/all_gather | solution.py:42
  323.9 25.5 %reduce-scatter.35.cloned.1.call-done = bf16[512,256]{1,0:T(8,128)(2,1)} async-done(((bf16[512,1024]{1,0:T(8,128)(2,1)}), bf16[512,256]{1,0:T(8,128)(2,1)}) %reduce-scatter.35.cloned.1.call-update) | async-done | bytes 262160 | tf_op jit(solution)/shard_map/reduce_scatter | solution.py:46
  364.5 25.2 %all-gather.38.cloned.1.call-done = bf16[512,1024]{1,0:T(8,128)(2,1)} async-done(((bf16[512,256]{1,0:T(8,128)(2,1)}), bf16[512,1024]{1,0:T(8,128)(2,1)}) %all-gather.38.cloned.1.call-update) | async-done | bytes 1048592 | tf_op jit(solution)/shard_map/all_gather | solution.py:42
  424.6 25.8 %all-gather.48.cloned.1.call-done = bf16[512,1024]{1,0:T(8,128)(2,1)} async-done(((bf16[512,256]{1,0:T(8,128)(2,1)}), bf16[512,1024]{1,0:T(8,128)(2,1)}) %all-gather.48.cloned.1.call-update) | async-done | bytes 1048592 | tf_op jit(solution)/shard_map/all_gather | solution.py:52
  478.9 28.6 %reduce-scatter.37.cloned.1.call-done = bf16[512,256]{1,0:T(8,128)(2,1)} async-done(((bf16[512,1024]{1,0:T(8,128)(2,1)}), bf16[512,256]{1,0:T(8,128)(2,1)}) %reduce-scatter.37.cloned.1.call-update) | async-done | bytes 262160 | tf_op jit(solution)/shard_map/reduce_scatter | solution.py:56
  520.8 28.8 %all-gather.40.cloned.1.call-done = bf16[512,1024]{1,0:T(8,128)(2,1)} async-done(((bf16[512,256]{1,0:T(8,128)(2,1)}), bf16[512,1024]{1,0:T(8,128)(2,1)}) %all-gather.40.cloned.1.call-update) | async-done | bytes 1048592 | tf_op jit(solution)/shard_map/all_gather | solution.py:42
  555.7 25.7 %reduce-scatter.29.cloned.1.call-done = bf16[512,256]{1,0:T(8,128)(2,1)} async-done(((bf16[512,1024]{1,0:T(8,128)(2,1)}), bf16[512,256]{1,0:T(8,128)(2,1)}) %reduce-scatter.29.cloned.1.call-update) | async-done | bytes 262160 | tf_op jit(solution)/shard_map/reduce_scatter | solution.py:46
  597.1 28.5 %all-gather.52.cloned.1.call-done = bf16[512,1024]{1,0:T(8,128)(2,1)} async-done(((bf16[512,256]{1,0:T(8,128)(2,1)}), bf16[512,1024]{1,0:T(8,128)(2,1)}) %all-gather.52.cloned.1.call-update) | async-done | bytes 1048592 | tf_op jit(solution)/shard_map/all_gather | solution.py:52
  637.4 25.7 %reduce-scatter.39.cloned.1.call-done = bf16[512,256]{1,0:T(8,128)(2,1)} async-done(((bf16[512,1024]{1,0:T(8,128)(2,1)}), bf16[512,256]{1,0:T(8,128)(2,1)}) %reduce-scatter.39.cloned.1.call-update) | async-done | bytes 262160 | tf_op jit(solution)/shard_map/reduce_scatter | solution.py:56
  666.0 28.4 %all-gather.54.cloned.1.call-done = bf16[512,1024]{1,0:T(8,128)(2,1)} async-done(((bf16[512,256]{1,0:T(8,128)(2,1)}), bf16[512,1024]{1,0:T(8,128)(2,1)}) %all-gather.54.cloned.1.call-update) | async-done | bytes 1048592 | tf_op jit(solution)/shard_map/all_gather | solution.py:42
  702.5 25.7 %reduce-scatter.41.cloned.1.call-done = bf16[512,256]{1,0:T(8,128)(2,1)} async-done(((bf16[512,1024]{1,0:T(8,128)(2,1)}), bf16[512,256]{1,0:T(8,128)(2,1)}) %reduce-scatter.41.cloned.1.call-update) | async-done | bytes 262160 | tf_op jit(solution)/shard_map/reduce_scatter | solution.py:46
  754.9 19.9 %all-gather.62.cloned.1.call-done = bf16[512,1024]{1,0:T(8,128)(2,1)} async-done(((bf16[512,256]{1,0:T(8,128)(2,1)}), bf16[512,1024]{1,0:T(8,128)(2,1)}) %all-gather.62.cloned.1.call-update) | async-done | bytes 1048592 | tf_op jit(solution)/shard_map/all_gather | solution.py:42
  782.9 22.3 %all-gather.58.cloned.1.call-done = bf16[512,1024]{1,0:T(8,128)(2,1)} async-done(((bf16[512,256]{1,0:T(8,128)(2,1)}), bf16[512,1024]{1,0:T(8,128)(2,1)}) %all-gather.58.cloned.1.call-update) | async-done | bytes 1048592 | tf_op jit(solution)/shard_map/all_gather | solution.py:42
  809.7 25.8 %all-gather.56.cloned.1.call-done = bf16[512,1024]{1,0:T(8,128)(2,1)} async-done(((bf16[512,256]{1,0:T(8,128)(2,1)}), bf16[512,1024]{1,0:T(8,128)(2,1)}) %all-gather.56.cloned.1.call-update) | async-done | bytes 1048592 | tf_op jit(solution)/shard_map/all_gather | solution.py:52
  863.9 28.7 %reduce-scatter.43.cloned.1.call-done = bf16[512,256]{1,0:T(8,128)(2,1)} async-done(((bf16[512,1024]{1,0:T(8,128)(2,1)}), bf16[512,256]{1,0:T(8,128)(2,1)}) %reduce-scatter.43.cloned.1.call-update) | async-done | bytes 262160 | tf_op jit(solution)/shard_map/reduce_scatter | solution.py:56
  907.1 28.3 %all-gather.60.cloned.1.call-done = bf16[512,1024]{1,0:T(8,128)(2,1)} async-done(((bf16[512,256]{1,0:T(8,128)(2,1)}), bf16[512,1024]{1,0:T(8,128)(2,1)}) %all-gather.60.cloned.1.call-update) | async-done | bytes 1048592 | tf_op jit(solution)/shard_map/all_gather | solution.py:52
  947.3 25.7 %reduce-scatter.45.cloned.1.call-done = bf16[512,256]{1,0:T(8,128)(2,1)} async-done(((bf16[512,1024]{1,0:T(8,128)(2,1)}), bf16[512,256]{1,0:T(8,128)(2,1)}) %reduce-scatter.45.cloned.1.call-update) | async-done | bytes 262160 | tf_op jit(solution)/shard_map/reduce_scatter | solution.py:56
  1001.1 20.1 %all-gather.42.cloned.1.call-done = bf16[512,1024]{1,0:T(8,128)(2,1)} async-done(((bf16[512,256]{1,0:T(8,128)(2,1)}), bf16[512,1024]{1,0:T(8,128)(2,1)}) %all-gather.42.cloned.1.call-update) | async-done | bytes 1048592 | tf_op jit(solution)/shard_map/all_gather | solution.py:42
  1056.1 25.2 %all-gather.64.cloned.1.call-done = bf16[512,1024]{1,0:T(8,128)(2,1)} async-done(((bf16[512,256]{1,0:T(8,128)(2,1)}), bf16[512,1024]{1,0:T(8,128)(2,1)}) %all-gather.64.cloned.1.call-update) | async-done | bytes 1048592 | tf_op jit(solution)/shard_map/all_gather | solution.py:52
  1088.8 20.9 %reduce-scatter.31.cloned.1.call-done = bf16[512,256]{1,0:T(8,128)(2,1)} async-done(((bf16[512,1024]{1,0:T(8,128)(2,1)}), bf16[512,256]{1,0:T(8,128)(2,1)}) %reduce-scatter.31.cloned.1.call-update) | async-done | bytes 262160 | tf_op jit(solution)/shard_map/reduce_scatter | solution.py:46
  1109.7 28.7 %reduce-scatter.49.cloned.1.call-done = bf16[512,256]{1,0:T(8,128)(2,1)} async-done(((bf16[512,1024]{1,0:T(8,128)(2,1)}), bf16[512,256]{1,0:T(8,128)(2,1)}) %reduce-scatter.49.cloned.1.call-update) | async-done | bytes 262160 | tf_op jit(solution)/shard_map/reduce_scatter | solution.py:56
  1151.4 28.8 %all-gather.68.cloned.1.call-done = bf16[512,1024]{1,0:T(8,128)(2,1)} async-done(((bf16[512,256]{1,0:T(8,128)(2,1)}), bf16[512,1024]{1,0:T(8,128)(2,1)}) %all-gather.68.cloned.1.call-update) | async-done | bytes 1048592 | tf_op jit(solution)/shard_map/all_gather | solution.py:52
  1257.0 24.2 %reduce-scatter.57.cloned.1.call-done = bf16[256,1024]{1,0:T(8,128)(2,1)} async-done(((bf16[1024,1024]{1,0:T(8,128)(2,1)}), bf16[256,1024]{1,0:T(8,128)(2,1)}) %reduce-scatter.57.cloned.1.call-update) | async-done | bytes 524304 | tf_op jit(solution)/shard_map/reduce_scatter | solution.py:342
  1283.3 29.8 %all-gather.44.cloned.1.call-done = bf16[512,1024]{1,0:T(8,128)(2,1)} async-done(((bf16[512,256]{1,0:T(8,128)(2,1)}), bf16[512,1024]{1,0:T(8,128)(2,1)}) %all-gather.44.cloned.1.call-update) | async-done | bytes 1048592 | tf_op jit(solution)/shard_map/all_gather | solution.py:42
  1319.2 30.4 %reduce-scatter.59.cloned.1.call-done = bf16[1024,256]{1,0:T(8,128)(2,1)} async-done(((bf16[1024,1024]{1,0:T(8,128)(2,1)}), bf16[1024,256]{1,0:T(8,128)(2,1)}) %reduce-scatter.59.cloned.1.call-update) | async-done | bytes 524304 | tf_op jit(solution)/shard_map/reduce_scatter | solution.py:348
  1351.7 25.7 %reduce-scatter.55.cloned.1.call-done = bf16[4,64,256]{2,1,0:T(8,128)(2,1)} async-done(((bf16[4,64,1024]{2,1,0:T(8,128)(2,1)}), bf16[4,64,256]{2,1,0:T(8,128)(2,1)}) %reduce-scatter.55.cloned.1.call-update) | async-done | bytes 131088 | tf_op jit(solution)/shard_map/reduce_scatter | solution.py:330
  1413.5 27.7 %reduce-scatter.33.cloned.1.call-done = bf16[512,256]{1,0:T(8,128)(2,1)} async-done(((bf16[512,1024]{1,0:T(8,128)(2,1)}), bf16[512,256]{1,0:T(8,128)(2,1)}) %reduce-scatter.33.cloned.1.call-update) | async-done | bytes 262160 | tf_op jit(solution)/shard_map/reduce_scatter | solution.py:46
  (513 shorter events, 572.1 us)
Async XLA Ops:
  41.5 94.4 %reduce-scatter.23.cloned.1.call-start = ((), (), s32[]{:S(2)}) async-start(), calls=%async_computation.21 | async-start | bytes 1310720 | tf_op jit(solution)/shard_map/reduce_scatter | solution.py:46
  109.1 99.0 %all-gather.72.cloned.1.call-start = ((), (), s32[]{:S(2)}) async-start(), calls=%async_computation.58 | async-start | bytes 2621440 | tf_op jit(solution)/shard_map/all_gather | solution.py:248
  109.7 130.4 %all-gather.36.cloned.1.call-start = ((), (), s32[]{:S(2)}) async-start(), calls=%async_computation.22 | async-start | bytes 1310720 | tf_op jit(solution)/shard_map/all_gather | solution.py:42
  148.3 123.6 %reduce-scatter.25.cloned.1.call-start = ((), (), s32[]{:S(2)}) async-start(), calls=%async_computation.23 | async-start | bytes 1310720 | tf_op jit(solution)/shard_map/reduce_scatter | solution.py:46
  246.2 68.7 %all-gather.46.cloned.1.call-start = ((), (), s32[]{:S(2)}) async-start(), calls=%async_computation.32 | async-start | bytes 1310720 | tf_op jit(solution)/shard_map/all_gather | solution.py:42
  286.2 63.2 %reduce-scatter.35.cloned.1.call-start = ((), (), s32[]{:S(2)}) async-start(), calls=%async_computation.33 | async-start | bytes 1310720 | tf_op jit(solution)/shard_map/reduce_scatter | solution.py:46
  323.6 66.1 %all-gather.38.cloned.1.call-start = ((), (), s32[]{:S(2)}) async-start(), calls=%async_computation.24 | async-start | bytes 1310720 | tf_op jit(solution)/shard_map/all_gather | solution.py:42
  362.9 87.5 %all-gather.48.cloned.1.call-start = ((), (), s32[]{:S(2)}) async-start(), calls=%async_computation.34 | async-start | bytes 1310720 | tf_op jit(solution)/shard_map/all_gather | solution.py:52
  364.3 114.6 %reduce-scatter.27.cloned.1.call-start = ((), (), s32[]{:S(2)}) async-start(), calls=%async_computation.25 | async-start | bytes 1310720 | tf_op jit(solution)/shard_map/reduce_scatter | solution.py:46
  402.9 104.5 %reduce-scatter.37.cloned.1.call-start = ((), (), s32[]{:S(2)}) async-start(), calls=%async_computation.36 | async-start | bytes 1310720 | tf_op jit(solution)/shard_map/reduce_scatter | solution.py:56
  459.4 90.1 %all-gather.40.cloned.1.call-start = ((), (), s32[]{:S(2)}) async-start(), calls=%async_computation.26 | async-start | bytes 1310720 | tf_op jit(solution)/shard_map/all_gather | solution.py:42
  555.7 69.9 %all-gather.52.cloned.1.call-start = ((), (), s32[]{:S(2)}) async-start(), calls=%async_computation.37 | async-start | bytes 1310720 | tf_op jit(solution)/shard_map/all_gather | solution.py:52
  596.8 66.3 %reduce-scatter.39.cloned.1.call-start = ((), (), s32[]{:S(2)}) async-start(), calls=%async_computation.38 | async-start | bytes 1310720 | tf_op jit(solution)/shard_map/reduce_scatter | solution.py:56
  702.4 72.4 %all-gather.62.cloned.1.call-start = ((), (), s32[]{:S(2)}) async-start(), calls=%async_computation.46 | async-start | bytes 1310720 | tf_op jit(solution)/shard_map/all_gather | solution.py:42
  748.5 87.0 %all-gather.56.cloned.1.call-start = ((), (), s32[]{:S(2)}) async-start(), calls=%async_computation.41 | async-start | bytes 1310720 | tf_op jit(solution)/shard_map/all_gather | solution.py:52
  754.6 109.3 %reduce-scatter.47.cloned.1.call-start = ((), (), s32[]{:S(2)}) async-start(), calls=%async_computation.47 | async-start | bytes 1310720 | tf_op jit(solution)/shard_map/reduce_scatter | solution.py:46
  782.9 109.7 %reduce-scatter.43.cloned.1.call-start = ((), (), s32[]{:S(2)}) async-start(), calls=%async_computation.43 | async-start | bytes 1310720 | tf_op jit(solution)/shard_map/reduce_scatter | solution.py:56
  844.7 90.8 %all-gather.60.cloned.1.call-start = ((), (), s32[]{:S(2)}) async-start(), calls=%async_computation.44 | async-start | bytes 1310720 | tf_op jit(solution)/shard_map/all_gather | solution.py:52
  906.6 66.4 %reduce-scatter.45.cloned.1.call-start = ((), (), s32[]{:S(2)}) async-start(), calls=%async_computation.45 | async-start | bytes 1310720 | tf_op jit(solution)/shard_map/reduce_scatter | solution.py:56
  947.2 74.0 %all-gather.42.cloned.1.call-start = ((), (), s32[]{:S(2)}) async-start(), calls=%async_computation.28 | async-start | bytes 1310720 | tf_op jit(solution)/shard_map/all_gather | solution.py:42
  994.6 86.6 %all-gather.64.cloned.1.call-start = ((), (), s32[]{:S(2)}) async-start(), calls=%async_computation.48 | async-start | bytes 1310720 | tf_op jit(solution)/shard_map/all_gather | solution.py:52
  1000.8 108.9 %reduce-scatter.31.cloned.1.call-start = ((), (), s32[]{:S(2)}) async-start(), calls=%async_computation.29 | async-start | bytes 1310720 | tf_op jit(solution)/shard_map/reduce_scatter | solution.py:46
  1034.3 104.1 %reduce-scatter.49.cloned.1.call-start = ((), (), s32[]{:S(2)}) async-start(), calls=%async_computation.50 | async-start | bytes 1310720 | tf_op jit(solution)/shard_map/reduce_scatter | solution.py:56
  1088.7 91.4 %all-gather.68.cloned.1.call-start = ((), (), s32[]{:S(2)}) async-start(), calls=%async_computation.51 | async-start | bytes 1310720 | tf_op jit(solution)/shard_map/all_gather | solution.py:52
  1151.4 66.4 %reduce-scatter.51.cloned.1.call-start = ((), (), s32[]{:S(2)}) async-start(), calls=%async_computation.52 | async-start | bytes 1310720 | tf_op jit(solution)/shard_map/reduce_scatter | solution.py:56
  1192.0 63.6 %reduce-scatter.61.cloned.1.call-start = ((), (), s32[]{:S(2)}) async-start(), calls=%async_computation.60 | async-start | bytes 40960
  1199.8 81.4 %reduce-scatter.57.cloned.1.call-start = ((), (), s32[]{:S(2)}) async-start(), calls=%async_computation.55 | async-start | bytes 2621440 | tf_op jit(solution)/shard_map/reduce_scatter | solution.py:342
  1205.0 108.1 %all-gather.44.cloned.1.call-start = ((), (), s32[]{:S(2)}) async-start(), calls=%async_computation.30 | async-start | bytes 1310720 | tf_op jit(solution)/shard_map/all_gather | solution.py:42
  1229.5 120.1 %reduce-scatter.59.cloned.1.call-start = ((), (), s32[]{:S(2)}) async-start(), calls=%async_computation.56 | async-start | bytes 2621440 | tf_op jit(solution)/shard_map/reduce_scatter | solution.py:348
  1238.4 139.1 %reduce-scatter.55.cloned.1.call-start = ((), (), s32[]{:S(2)}) async-start(), calls=%async_computation.54 | async-start | bytes 655360 | tf_op jit(solution)/shard_map/reduce_scatter | solution.py:330
  1245.5 166.0 %reduce-scatter.53.cloned.1.call-start = ((), (), s32[]{:S(2)}) async-start(), calls=%async_computation.53 | async-start | bytes 1966080 | tf_op jit(solution)/shard_map/reduce_scatter | solution.py:324
  1252.1 189.0 %reduce-scatter.33.cloned.1.call-start = ((), (), s32[]{:S(2)}) async-start(), calls=%async_computation.31 | async-start | bytes 1310720 | tf_op jit(solution)/shard_map/reduce_scatter | solution.py:46
  (116 other events, 3701.3 us)
Sparse Core Ops, SparseCore 0:
  40.9 26.1 all-gather.33
  68.9 28.9 all-gather.69
  108.6 27.2 reduce-scatter.22
  137.6 33.5 all-gather.73
  172.9 35.1 all-gather.71
  210.1 29.9 all-gather.35
  246.3 25.5 reduce-scatter.24
  286.3 28.5 all-gather.45
  323.8 25.5 reduce-scatter.34
  361.0 28.6 all-gather.37
  391.9 28.2 all-gather.49
  422.1 28.2 all-gather.47
  481.6 25.7 reduce-scatter.36
  520.9 28.6 all-gather.39
  555.8 25.5 reduce-scatter.28
  596.9 28.5 all-gather.51
  665.8 28.4 all-gather.53
  746.7 28.0 all-gather.61
  776.9 28.2 all-gather.57
  807.3 28.2 all-gather.55
  866.8 25.7 reduce-scatter.42
  906.7 28.6 all-gather.59
  993.1 28.0 all-gather.41
  1023.3 28.2 all-gather.65
  1053.0 28.2 all-gather.63
  1112.6 25.7 reduce-scatter.48
  1151.5 28.6 all-gather.67
  1245.9 35.1 reduce-scatter.56
  1283.1 29.9 all-gather.43
  1316.1 33.4 reduce-scatter.58
  1380.4 31.0 reduce-scatter.52
  1413.8 27.2 reduce-scatter.32
  (9 shorter events, 226.2 us)
where the time goes:
time: 1460 us; the launch traced here: 1450 us
  waiting for transfers between devices  991 us (68%)
  blocking collectives  168 us (12%)
  matrix products  166 us (11%)
  other arithmetic  73.8 us (5%)
  local copies, waits for them, and re-layouts  24.1 us (2%)
  between operations  18.7 us (1%)
    all_gather x12, waiting for transfers between devices, full_rows(): return lax.all_gather(piece, 'tensor', axis=1, tiled=True)  273 us
    reduce_scatter x9, waiting for transfers between devices, head_sums(): lax.psum_scatter(partial_rows.astype(jnp.bfloat16), 'tensor', scatter_dim...  216 us
    all_gather x6, waiting for transfers between devices, grad_full(): return lax.all_gather(piece, 'tensor', axis=1, tiled=True)  162 us
    reduce_scatter x6, waiting for transfers between devices, back_sums(): lax.psum_scatter(partial_rows.astype(jnp.bfloat16), 'tensor', scatter_dim...  150 us
    psum x11, blocking collectives, row_totals(): return lax.psum((jnp.sum(first, axis=1), jnp.sum(second, axis=1)), 'tensor')  120 us
    all_gather x1, waiting for transfers between devices, body(): lax.all_gather(up_weight[0], 'seq', axis=0, tiled=True)  36.9 us
    all_gather x1, waiting for transfers between devices, body(): lax.all_gather(qkv_weight[0], 'seq', axis=0, tiled=True)  30.9 us
    reduce_scatter x1, waiting for transfers between devices, body(): lax.psum_scatter(totals[10].astype(jnp.bfloat16), 'seq', scatter_dimensio...  30.4 us
  transfers between devices with their start and end apart: 45, of which 44 were waited for; matrix products, arithmetic and copies ran while one was open for 10% of the time, Pallas kernels for 0%

commit v1 on v0

v1 whole, which is shorter than its diff:
```python
import functools
import math

import jax
import jax.numpy as jnp
from jax import lax
from jax.sharding import PartitionSpec as P

epsilon = 1e-05
floor_value = -1e30
f32 = jnp.float32
bf16 = jnp.bfloat16


def gather_columns(piece):
    return lax.all_gather(piece, "tensor", axis=1, tiled=True)


def gather_rows(piece):
    return lax.all_gather(piece, "tensor", axis=0, tiled=True)


def scatter_rows(partial_rows):
    return lax.psum_scatter(
        partial_rows.astype(bf16), "tensor", scatter_dimension=0, tiled=True
    ).astype(f32)


def norm_parts(rows):
    average = jnp.mean(rows, axis=1, keepdims=True)
    variance = jnp.mean(rows * rows, axis=1, keepdims=True) - average * average
    scale = lax.rsqrt(variance + epsilon)
    return ((rows - average) * scale, scale)


def norm_backward(grad, centred, scale, gain):
    scaled = grad * gain
    total = jnp.mean(scaled, axis=1, keepdims=True)
    along = jnp.mean(scaled * centred, axis=1, keepdims=True)
    return scale * (scaled - total - centred * along)


def allowed_mask(segment):
    length = segment.shape[1]
    place = lax.broadcasted_iota(jnp.int32, (length, length), 0)
    other = lax.broadcasted_iota(jnp.int32, (length, length), 1)
    same = segment[:, :, None] == segment[:, None, :]
    return (same & (other <= place)[None])[:, None]


def gelu_value(upper):
    return jax.nn.gelu(upper, approximate=True)


def dot(left, right, dims):
    return lax.dot_general(left, right, (dims, ((), ())), preferred_element_type=f32)


def forward(whole, rows, mask, weights):
    gain1, bias1, w_qkv, b_qv, w_out, b_out, gain2, bias2, w_up, b_up, w_down, b_down = weights
    count = whole.shape[0]
    heads, wide = w_qkv.shape[1:]
    size = wide // 3
    shape4 = (mask.shape[0], mask.shape[2], heads, size)
    factor = 1.0 / math.sqrt(size)
    normed = (norm_parts(whole.astype(f32))[0] * gain1 + bias1).astype(bf16)
    rows = rows.astype(f32)
    centred1, scale1 = norm_parts(rows)
    mixed = jnp.einsum("rd,dhe->rhe", normed, w_qkv, preferred_element_type=f32)
    query = (mixed[..., :size] + b_qv[:, :size]).astype(bf16).reshape(shape4)
    keys = mixed[..., size : 2 * size].astype(bf16).reshape(shape4)
    values = (mixed[..., 2 * size :] + b_qv[:, size:]).astype(bf16).reshape(shape4)
    scores = jnp.einsum("sqhe,skhe->shqk", query, keys, preferred_element_type=f32) * factor
    masked = jnp.where(mask, scores, floor_value)
    raised = jnp.exp(masked - jnp.max(masked, axis=-1, keepdims=True))
    chance = raised / jnp.sum(raised, axis=-1, keepdims=True)
    low = chance.astype(bf16)
    context = jnp.einsum("shqk,skhe->sqhe", low, values, preferred_element_type=f32)
    context = context.reshape(count, heads * size).astype(bf16)
    attn = scatter_rows(dot(context, w_out, ((1,), (0,)))) + b_out
    hidden = rows + attn
    centred2, scale2 = norm_parts(hidden)
    normed2 = gather_rows((centred2 * gain2 + bias2).astype(bf16))
    upper = dot(normed2, w_up, ((1,), (0,))) + b_up
    active = gelu_value(upper).astype(bf16)
    branch = scatter_rows(dot(active, w_down, ((1,), (0,)))) + b_down
    output = (hidden + branch).astype(bf16)
    kept = (
        centred1, scale1, normed, query, keys, values, chance, low, context,
        centred2, scale2, normed2, upper, active,
    )
    return (output, kept)


def backward(grad_whole, grad_rows, weights, kept):
    gain1, bias1, w_qkv, b_qv, w_out, b_out, gain2, bias2, w_up, b_up, w_down, b_down = weights
    (
        centred1, scale1, normed, query, keys, values, chance, low, context,
        centred2, scale2, normed2, upper, active,
    ) = kept
    count = grad_whole.shape[0]
    heads, wide = w_qkv.shape[1:]
    size = wide // 3
    factor = 1.0 / math.sqrt(size)
    grad_out = grad_rows.astype(f32)
    grad_active = dot(grad_whole, w_down, ((1,), (1,)))
    grad_upper = jax.vjp(gelu_value, upper)[1](grad_active)[0].astype(bf16)
    grad_normed2 = scatter_rows(dot(grad_upper, w_up, ((1,), (1,))))
    grad_down = dot(active, grad_whole, ((0,), (0,)))
    grad_up = dot(normed2, grad_upper, ((0,), (0,)))
    grad_hidden = grad_out + norm_backward(grad_normed2, centred2, scale2, gain2)
    grad_attn = grad_hidden.astype(bf16)
    attn_whole = gather_rows(grad_attn)
    grad_context = dot(attn_whole, w_out, ((1,), (1,))).astype(bf16).reshape(query.shape)
    grad_out_w = dot(context, attn_whole, ((0,), (0,)))
    grad_chance = jnp.einsum("sqhe,skhe->shqk", grad_context, values, preferred_element_type=f32)
    delta = jnp.sum(grad_chance * chance, axis=-1, keepdims=True)
    grad_scores = (chance * (grad_chance - delta)).astype(bf16)
    grad_query = (
        jnp.einsum("shqk,skhe->sqhe", grad_scores, keys, preferred_element_type=f32) * factor
    ).astype(bf16)
    grad_keys = (
        jnp.einsum("shqk,sqhe->skhe", grad_scores, query, preferred_element_type=f32) * factor
    ).astype(bf16)
    grad_values = jnp.einsum(
        "shqk,sqhe->skhe", low, grad_context, preferred_element_type=f32
    ).astype(bf16)
    grad_mixed = jnp.concatenate([grad_query, grad_keys, grad_values], axis=-1).reshape(
        count, heads, wide
    )
    grad_normed1 = scatter_rows(
        jnp.einsum("rhe,dhe->rd", grad_mixed, w_qkv, preferred_element_type=f32)
    )
    grad_qkv = jnp.einsum("rd,rhe->dhe", normed, grad_mixed, preferred_element_type=f32)
    grad_qv = jnp.concatenate(
        [
            jnp.sum(grad_query.astype(f32), axis=(0, 1)),
            jnp.sum(grad_values.astype(f32), axis=(0, 1)),
        ],
        axis=-1,
    )
    grad_input = grad_hidden + norm_backward(grad_normed1, centred1, scale1, gain1)
    vectors = (
        jnp.sum(grad_normed1 * centred1, axis=0),
        jnp.sum(grad_normed1, axis=0),
        jnp.sum(grad_attn.astype(f32), axis=0),
        jnp.sum(grad_normed2 * centred2, axis=0),
        jnp.sum(grad_normed2, axis=0),
        jnp.sum(grad_out, axis=0),
    )
    local = (jnp.sum(grad_upper.astype(f32), axis=0), grad_qv)
    return (grad_input.astype(bf16), (grad_qkv, grad_out_w, grad_up, grad_down), vectors, local)


def swap(item):
    return lax.ppermute(item, "section", [(0, 1), (1, 0)])


def body(
    tokens,
    segments,
    cotangent,
    norm1_gain,
    norm1_bias,
    qkv_weight,
    qv_bias,
    out_weight,
    out_bias,
    norm2_gain,
    norm2_bias,
    up_weight,
    up_bias,
    down_weight,
    down_bias,
):
    section = lax.axis_index("section")
    place = lax.axis_index("tensor")
    tensors = lax.axis_size("tensor")
    quads = lax.axis_size("seq")
    first = section == 0
    rows_all, width = tokens.shape
    count = rows_all // 2
    block = count // tensors
    full = width * tensors
    heads, wide = qkv_weight.shape[2:]
    size = wide // 3
    part = norm1_gain.shape[1]
    part_up = up_bias.shape[1]
    part_qv = qv_bias.shape[2]

    def mine(item):
        return lax.dynamic_slice_in_dim(item, section * (item.shape[0] // 2), item.shape[0] // 2, 0)

    def block_of(whole):
        return lax.dynamic_slice_in_dim(whole, place * block, block, 0)

    def columns_of(whole):
        return lax.dynamic_slice_in_dim(whole, place * width, width, 1)

    whole0 = gather_columns(mine(tokens))
    packed = jnp.concatenate(
        [
            norm1_gain[0], norm1_bias[0], out_bias[0], norm2_gain[0], norm2_bias[0], down_bias[0],
            up_bias[0], qv_bias[0].reshape(-1),
        ]
    )
    small = lax.all_gather(packed, ("section", "tensor", "seq"), axis=0, tiled=False)
    small = small.reshape(2, tensors, quads, packed.shape[0]).astype(f32)

    def pair(weight, axis):
        gathered = lax.all_gather(weight, "seq", axis=axis, tiled=True)
        return lax.all_gather(gathered, "section", axis=0, tiled=False)

    w_qkv = pair(qkv_weight[0], 0)
    w_out = pair(out_weight[0].reshape(heads * size, -1), 1)
    w_up = pair(up_weight[0], 0)
    w_down = pair(down_weight[0], 1)
    whole_cot = gather_columns(mine(cotangent))

    def weights_of(layer):
        own = small[layer]
        vectors = [own[:, :, i * part : (i + 1) * part].reshape(full) for i in range(6)]
        local = lax.dynamic_slice_in_dim(own, place, 1, 0)[0]
        b_up = local[:, 6 * part : 6 * part + part_up].reshape(-1)
        b_qv = local[:, 6 * part + part_up :].reshape(quads, heads, part_qv)
        b_qv = jnp.transpose(b_qv, (1, 0, 2)).reshape(heads, 2 * size)
        return (
            vectors[0], vectors[1], w_qkv[layer], b_qv, w_out[layer], vectors[2],
            vectors[3], vectors[4], w_up[layer], b_up, w_down[layer], vectors[5],
        )

    params = (weights_of(0), weights_of(1))
    mask = allowed_mask(mine(segments))
    out0, kept0 = forward(whole0, block_of(whole0), mask, params[0])
    whole1 = gather_rows(out0)
    out1, kept1 = forward(whole1, out0, mask, params[1])
    grad1, big1, vec1, loc1 = backward(whole_cot, block_of(whole_cot), params[1], kept1)

    def reduce_big(big):
        axes = (0, 1, 0, 1)
        return tuple(
            lax.psum_scatter(item.astype(bf16), "seq", scatter_dimension=axis, tiled=True)
            for item, axis in zip(big, axes)
        )

    red1 = reduce_big(big1)
    whole_grad = gather_rows(grad1)
    grad0, big0, vec0, loc0 = backward(whole_grad, grad1, params[0], kept0)
    red0 = reduce_big(big0)

    def to_columns(rows):
        return lax.all_to_all(rows, "tensor", split_axis=1, concat_axis=0, tiled=True)

    def settle(of0, of1):
        own = jnp.where(first, of0, of1)
        other = swap(jnp.where(first, of1, of0))
        return jnp.where(
            first, jnp.concatenate([own, other]), jnp.concatenate([other, own])
        )

    outputs = settle(columns_of(whole1), to_columns(out1))
    input_grads = settle(to_columns(grad0), columns_of(whole_grad))
    totals = tuple(
        jnp.where(first, a, b).astype(f32) + swap(jnp.where(first, b, a)).astype(f32)
        for a, b in zip(red0, red1)
    )

    def pack(vectors, local):
        rows = [item.reshape(tensors, quads, part) for item in vectors]
        up = local[0].reshape(1, quads, part_up)
        qv = jnp.transpose(local[1].reshape(heads, quads, part_qv), (1, 0, 2))
        here = jnp.concatenate([up, qv.reshape(1, quads, heads * part_qv)], axis=-1)
        ours = lax.broadcasted_iota(jnp.int32, (tensors, 1, 1), 0) == place
        rows.append(jnp.where(ours, here, 0.0))
        return jnp.concatenate(rows, axis=-1)

    vectors = jnp.stack([pack(vec0, loc0), pack(vec1, loc1)])
    vectors = vectors.reshape(2 * tensors * quads, -1)
    vectors = lax.psum_scatter(
        vectors, ("section", "tensor", "seq"), scatter_dimension=0, tiled=True
    )[0]
    small_grads = [vectors[i * part : (i + 1) * part] for i in range(6)]
    g_up = vectors[6 * part : 6 * part + part_up]
    g_qv = vectors[6 * part + part_up :].reshape(heads, part_qv)
    result = (
        outputs,
        input_grads,
        small_grads[0],
        small_grads[1],
        totals[0],
        g_qv,
        totals[1].reshape(heads, size, -1),
        small_grads[2],
        small_grads[3],
        small_grads[4],
        totals[2],
        g_up,
        totals[3],
        small_grads[5],
    )
    return tuple(item[None] for item in result)


def solution(mesh):
    return jax.shard_map(
        body,
        mesh=mesh,
        in_specs=(
            P("seq", "tensor"),
            P("seq", None),
            P("seq", "tensor"),
            P("section", ("tensor", "seq")),
            P("section", ("tensor", "seq")),
            P("section", "seq", "tensor", None),
            P("section", "tensor", "seq"),
            P("section", "tensor", None, "seq"),
            P("section", ("tensor", "seq")),
            P("section", ("tensor", "seq")),
            P("section", ("tensor", "seq")),
            P("section", "seq", "tensor"),
            P("section", ("tensor", "seq")),
            P("section", "tensor", "seq"),
            P("section", ("tensor", "seq")),
        ),
        out_specs=(
            P("section", "seq", "tensor"),
            P("section", "seq", "tensor"),
            P("section", ("tensor", "seq")),
            P("section", ("tensor", "seq")),
            P("section", "seq", "tensor", None),
            P("section", "tensor", "seq"),
            P("section", "tensor", None, "seq"),
            P("section", ("tensor", "seq")),
            P("section", ("tensor", "seq")),
            P("section", ("tensor", "seq")),
            P("section", "seq", "tensor"),
            P("section", ("tensor", "seq")),
            P("section", "tensor", "seq"),
            P("section", ("tensor", "seq")),
        ),
        check_vma=False,
    )
```

time: 1460 us -> 1110 us (0.76)
  waiting for transfers between devices: 991 us -> 827 us
  blocking collectives: 168 us -> 80.2 us
  matrix products: 166 us -> 102 us
  other arithmetic: 73.8 us -> 48.3 us
    all_gather x21 -> x15, waiting for transfers between devices: 518 us -> 262 us  [the longest x6 144 us: gather_rows(): return lax.all_gather(piece, 'tensor', axis=0, tiled=True)]
    unnamed x42 -> x33, waiting for transfers between devices: 2.4 us -> 130 us
    psum x11 -> x0, blocking collectives: 120 us -> none  [row_totals(): return lax.psum((jnp.sum(first, axis=1), jnp.sum(second, axis=1)), 'tensor')]
    all_gather x3 -> x2, blocking collectives: 27.5 us -> 80.2 us  [the longest x1 66.5 us: body(): lax.all_gather(packed, ('section', 'tensor', 'seq'), axis=0, tiled=False)]
    dot_general x48 -> x26, matrix products: 123 us -> 77.8 us  [the longest x18 62.9 us: dot(): lax.dot_general(left, right, (dims, ((), ())), preferred_element_type=f32)]
    reduce_scatter x19 -> x16, waiting for transfers between devices: 464 us -> 426 us  [the longest x8 219 us: reduce_big(): lax.psum_scatter(item.astype(bf16), 'seq', scatter_dimension=axis, tiled=...]
    unnamed x2 -> x0, blocking collectives: 20.4 us -> none
    unnamed x224 -> x126, local copies, waits for them, and re-layouts: 23.9 us -> 6.1 us
  transfers between devices with their start and end apart: 45 -> 40, of which waited for: 44 -> 29; matrix products, arithmetic and copies ran while one was open for 10% -> 10% of each run, Pallas kernels for 0% -> 0%
where the time goes in v1:
time: 1110 us; the launch traced here: 1100 us
  waiting for transfers between devices  827 us (75%)
  matrix products  102 us (9%)
  blocking collectives  80.2 us (7%)
  other arithmetic  48.3 us (4%)
  local copies, waits for them, and re-layouts  21.9 us (2%)
  between operations  15.4 us (1%)
    reduce_scatter x8, waiting for transfers between devices, reduce_big(): lax.psum_scatter(item.astype(bf16), 'seq', scatter_dimension=axis, tiled=...  219 us
    reduce_scatter x8, waiting for transfers between devices, scatter_rows(): lax.psum_scatter(partial_rows.astype(bf16), 'tensor', scatter_dimension=0...  207 us
    all_gather x6, waiting for transfers between devices, gather_rows(): return lax.all_gather(piece, 'tensor', axis=0, tiled=True)  144 us
    unnamed x33, waiting for transfers between devices  130 us
    all_gather x3, waiting for transfers between devices, pair(): gathered = lax.all_gather(weight, 'seq', axis=axis, tiled=True)  66.6 us
    all_gather x1, blocking collectives, body(): lax.all_gather(packed, ('section', 'tensor', 'seq'), axis=0, tiled=False)  66.5 us
    dot_general x18, matrix products, dot(): lax.dot_general(left, right, (dims, ((), ())), preferred_element_type=f32)  62.9 us
    all_gather x2, waiting for transfers between devices, gather_columns(): return lax.all_gather(piece, 'tensor', axis=1, tiled=True)  26.8 us
  transfers between devices with their start and end apart: 40, of which 29 were waited for; matrix products, arithmetic and copies ran while one was open for 10% of the time, Pallas kernels for 0%

profile of v1, /device:TPU:0, one launch (start us, length us, event | category | flops | bytes accessed | tf_op | source)
XLA Modules:
  0.0 1104.1 jit_solution(2725057039113949337)
XLA Ops:
  9.0 34.3 %all-gather.41.cloned.1.call-done = bf16[1,1024,4,192]{1,3,2,0:T(8,128)(2,1)} async-done(((bf16[1,256,4,192]{1,3,2,0:T(8,128)(2,1)}), bf16[1,1024,4,192]{1,3,2,0:T(8,128)(2,1)}) %all-gather.41.cloned.1.call-update) | async-done | bytes 1572880 | tf_op jit(solution)/shard_map/all_gather | solution.py:211
  43.4 13.8 %all_gather.72 = bf16[256,1024]{1,0:T(8,128)(2,1)} all-gather(bf16[256,256]{1,0:T(8,128)(2,1)S(1)} %bitcast.220), channel_id=1, replica_groups=mesh['section'=2,'seq'=4,'tensor'=4] {'seq'}, dimensions={1}, use_global_device_ids=true | all-gather | bytes 655360 | tf_op jit(solution)/shard_map/all_gather | solution.py:211
  58.1 66.5 %all-gather.8 = bf16[32,1,768]{2,1,0:T(2,128)(2,1)S(1)} all-gather(bf16[1,1,768]{2,1,0:T(2,128)(2,1)S(1)} %reshape.655), channel_id=2, replica_groups=mesh['section'=2,'seq'=4,'tensor'=4] {'section','tensor','seq'}, dimensions={0}, use_global_device_ids=true | all-gather | bytes 50688 | tf_op jit(solution)/shard_map/all_gather | solution.py:207
  144.4 23.6 %reduce-scatter.17.cloned.1.call-done = bf16[128,1024]{1,0:T(8,128)(2,1)} async-done(((bf16[512,1024]{1,0:T(8,128)(2,1)}), bf16[128,1024]{1,0:T(8,128)(2,1)}) %reduce-scatter.17.cloned.1.call-update) | async-done | bytes 262160 | tf_op jit(solution)/shard_map/reduce_scatter | solution.py:24
  171.1 32.4 %all-gather.51.cloned.1.call-done = bf16[1,1024,1024]{2,1,0:T(8,128)(2,1)} async-done(((bf16[1,1024,256]{2,1,0:T(8,128)(2,1)}), bf16[1,1024,1024]{2,1,0:T(8,128)(2,1)}) %all-gather.51.cloned.1.call-update) | async-done | bytes 2097168 | tf_op jit(solution)/shard_map/all_gather | solution.py:211
  203.6 15.1 %all-gather.49.cloned.1.call-done = bf16[2,1024,1024]{2,1,0:T(8,128)(2,1)} async-done(((bf16[1,1024,1024]{2,1,0:T(8,128)(2,1)}), bf16[2,1024,1024]{2,1,0:T(8,128)(2,1)}) %all-gather.49.cloned.1.call-update) | async-done | bytes 4194320 | tf_op jit(solution)/shard_map/all_gather | solution.py:212
  218.7 31.3 %all-gather.27.cloned.1.call-done = bf16[512,1024]{1,0:T(8,128)(2,1)} async-done(((bf16[128,1024]{1,0:T(8,128)(2,1)}), bf16[512,1024]{1,0:T(8,128)(2,1)}) %all-gather.27.cloned.1.call-update) | async-done | bytes 1048592 | tf_op jit(solution)/shard_map/all_gather | solution.py:20
  254.6 10.0 all-gather.53.cloned.1.call-done
  269.4 28.5 %reduce-scatter.19.cloned.1.call-done = bf16[128,1024]{1,0:T(8,128)(2,1)} async-done(((bf16[512,1024]{1,0:T(8,128)(2,1)}), bf16[128,1024]{1,0:T(8,128)(2,1)}) %reduce-scatter.19.cloned.1.call-update) | async-done | bytes 262160 | tf_op jit(solution)/shard_map/reduce_scatter | solution.py:24
  300.5 25.9 %all-gather.29.cloned.1.call-done = bf16[512,1024]{1,0:T(8,128)(2,1)} async-done(((bf16[128,1024]{1,0:T(8,128)(2,1)}), bf16[512,1024]{1,0:T(8,128)(2,1)}) %all-gather.29.cloned.1.call-update) | async-done | bytes 1048592 | tf_op jit(solution)/shard_map/all_gather | solution.py:20
  341.2 26.5 %reduce-scatter.21.cloned.1.call-done = bf16[128,1024]{1,0:T(8,128)(2,1)} async-done(((bf16[512,1024]{1,0:T(8,128)(2,1)}), bf16[128,1024]{1,0:T(8,128)(2,1)}) %reduce-scatter.21.cloned.1.call-update) | async-done | bytes 262160 | tf_op jit(solution)/shard_map/reduce_scatter | solution.py:24
  371.7 25.7 %all-gather.31.cloned.1.call-done = bf16[512,1024]{1,0:T(8,128)(2,1)} async-done(((bf16[128,1024]{1,0:T(8,128)(2,1)}), bf16[512,1024]{1,0:T(8,128)(2,1)}) %all-gather.31.cloned.1.call-update) | async-done | bytes 1048592 | tf_op jit(solution)/shard_map/all_gather | solution.py:20
  401.9 26.8 %all-gather.33.cloned.1.call-done = bf16[512,1024]{1,0:T(8,128)(2,1)} async-done(((bf16[512,256]{1,0:T(8,128)(2,1)}), bf16[512,1024]{1,0:T(8,128)(2,1)}) %all-gather.33.cloned.1.call-update) | async-done | bytes 1048592 | tf_op jit(solution)/shard_map/all_gather | solution.py:16
  428.7 5.2 convert_reduce_fusion.2
  442.1 20.8 %reduce-scatter.25.cloned.1.call-done = bf16[128,1024]{1,0:T(8,128)(2,1)} async-done(((bf16[512,1024]{1,0:T(8,128)(2,1)}), bf16[128,1024]{1,0:T(8,128)(2,1)}) %reduce-scatter.25.cloned.1.call-update) | async-done | bytes 262160 | tf_op jit(solution)/shard_map/reduce_scatter | solution.py:24
  464.3 27.2 %reduce-scatter.23.cloned.1.call-done = bf16[128,1024]{1,0:T(8,128)(2,1)} async-done(((bf16[512,1024]{1,0:T(8,128)(2,1)}), bf16[128,1024]{1,0:T(8,128)(2,1)}) %reduce-scatter.23.cloned.1.call-update) | async-done | bytes 262160 | tf_op jit(solution)/shard_map/reduce_scatter | solution.py:24
  494.0 26.4 %all-gather.35.cloned.1.call-done = bf16[512,1024]{1,0:T(8,128)(2,1)} async-done(((bf16[128,1024]{1,0:T(8,128)(2,1)}), bf16[512,1024]{1,0:T(8,128)(2,1)}) %all-gather.35.cloned.1.call-update) | async-done | bytes 1048592 | tf_op jit(solution)/shard_map/all_gather | solution.py:20
  532.3 26.8 %reduce-scatter.27.cloned.1.call-done = bf16[128,1024]{1,0:T(8,128)(2,1)} async-done(((bf16[512,1024]{1,0:T(8,128)(2,1)}), bf16[128,1024]{1,0:T(8,128)(2,1)}) %reduce-scatter.27.cloned.1.call-update) | async-done | bytes 262160 | tf_op jit(solution)/shard_map/reduce_scatter | solution.py:24
  562.3 26.6 %all-gather.37.cloned.1.call-done = bf16[512,1024]{1,0:T(8,128)(2,1)} async-done(((bf16[128,1024]{1,0:T(8,128)(2,1)}), bf16[512,1024]{1,0:T(8,128)(2,1)}) %all-gather.37.cloned.1.call-update) | async-done | bytes 1048592 | tf_op jit(solution)/shard_map/all_gather | solution.py:20
  588.9 5.2 convert_reduce_fusion.3
  597.4 26.8 %reduce-scatter.29.cloned.1.call-done = bf16[128,1024]{1,0:T(8,128)(2,1)} async-done(((bf16[512,1024]{1,0:T(8,128)(2,1)}), bf16[128,1024]{1,0:T(8,128)(2,1)}) %reduce-scatter.29.cloned.1.call-update) | async-done | bytes 262160 | tf_op jit(solution)/shard_map/reduce_scatter | solution.py:24
  647.0 7.7 all-gather.39.cloned.1.call-done
  679.0 8.1 all-to-all-done
  696.4 33.9 %reduce-scatter.45.cloned.1.call-done = bf16[1024,256]{1,0:T(8,128)(2,1)} async-done(((bf16[1024,1024]{1,0:T(8,128)(2,1)}), bf16[1024,256]{1,0:T(8,128)(2,1)}) %reduce-scatter.45.cloned.1.call-update) | async-done | bytes 524304 | tf_op jit(solution)/shard_map/reduce_scatter | solution.py:242
  732.4 36.0 %reduce-scatter.43.cloned.1.call-done = bf16[256,1024]{1,0:T(8,128)(2,1)} async-done(((bf16[1024,1024]{1,0:T(8,128)(2,1)}), bf16[256,1024]{1,0:T(8,128)(2,1)}) %reduce-scatter.43.cloned.1.call-update) | async-done | bytes 524304 | tf_op jit(solution)/shard_map/reduce_scatter | solution.py:242
  768.4 38.0 %reduce-scatter.41.cloned.1.call-done = bf16[256,1024]{1,0:T(8,128)(2,1)} async-done(((bf16[1024,1024]{1,0:T(8,128)(2,1)}), bf16[256,1024]{1,0:T(8,128)(2,1)}) %reduce-scatter.41.cloned.1.call-update) | async-done | bytes 524304 | tf_op jit(solution)/shard_map/reduce_scatter | solution.py:242
  809.9 26.6 %reduce-scatter.31.cloned.1.call-done = bf16[128,1024]{1,0:T(8,128)(2,1)} async-done(((bf16[512,1024]{1,0:T(8,128)(2,1)}), bf16[128,1024]{1,0:T(8,128)(2,1)}) %reduce-scatter.31.cloned.1.call-update) | async-done | bytes 262160 | tf_op jit(solution)/shard_map/reduce_scatter | solution.py:24
  845.5 18.0 %reduce-scatter.39.cloned.1.call-done = bf16[256,256]{1,0:T(8,128)(2,1)} async-done(((bf16[256,1024]{1,0:T(8,128)(2,1)}), bf16[256,256]{1,0:T(8,128)(2,1)}) %reduce-scatter.39.cloned.1.call-update) | async-done | bytes 131088 | tf_op jit(solution)/shard_map/reduce_scatter | solution.py:242
  863.5 28.5 %reduce-scatter.37.cloned.1.call-done = bf16[256,256]{1,0:T(8,128)(2,1)} async-done(((bf16[256,1024]{1,0:T(8,128)(2,1)}), bf16[256,256]{1,0:T(8,128)(2,1)}) %reduce-scatter.37.cloned.1.call-update) | async-done | bytes 131088 | tf_op jit(solution)/shard_map/reduce_scatter | solution.py:242
  895.7 30.3 %reduce-scatter.35.cloned.1.call-done = bf16[256,4,192]{0,2,1:T(8,128)(2,1)} async-done(((bf16[1024,4,192]{0,2,1:T(8,128)(2,1)}), bf16[256,4,192]{0,2,1:T(8,128)(2,1)}) %reduce-scatter.35.cloned.1.call-update) | async-done | bytes 393232 | tf_op jit(solution)/shard_map/reduce_scatter | solution.py:242
  926.1 34.2 %reduce-scatter.33.cloned.1.call-done = bf16[256,4,192]{0,2,1:T(8,128)(2,1)} async-done(((bf16[1024,4,192]{0,2,1:T(8,128)(2,1)}), bf16[256,4,192]{0,2,1:T(8,128)(2,1)}) %reduce-scatter.33.cloned.1.call-update) | async-done | bytes 393232 | tf_op jit(solution)/shard_map/reduce_scatter | solution.py:242
  962.2 126.8 %all-reduce.3.cloned.1.call-done = f32[32,768]{1,0:T(8,128)} async-done(((f32[32,768]{1,0:T(8,128)}), f32[32,768]{1,0:T(8,128)}) %all-reduce.3.cloned.1.call-update) | async-done | bytes 98320
  (365 shorter events, 175.2 us)
Async XLA Ops:
  8.0 117.8 %all-gather.25.cloned.1.call-start = ((), (), s32[]{:S(2)}) async-start(), calls=%async_computation.18 | async-start | bytes 1310720 | tf_op jit(solution)/shard_map/all_gather | solution.py:16
  9.0 118.5 %all-gather.43.cloned.1.call-start = ((), (), s32[]{:S(2)}) async-start(), calls=%async_computation.43 | async-start | bytes 4718592 | tf_op jit(solution)/shard_map/all_gather | solution.py:212
  43.3 96.7 %all-gather.45.cloned.1.call-start = ((), (), s32[]{:S(2)}) async-start(), calls=%async_computation.44 | async-start | bytes 1572864 | tf_op jit(solution)/shard_map/all_gather | solution.py:212
  57.2 86.3 %all-gather.47.cloned.1.call-start = ((), (), s32[]{:S(2)}) async-start(), calls=%async_computation.45 | async-start | bytes 2621440 | tf_op jit(solution)/shard_map/all_gather | solution.py:211
  57.8 110.3 %reduce-scatter.17.cloned.1.call-start = ((), (), s32[]{:S(2)}) async-start(), calls=%async_computation.19 | async-start | bytes 1310720 | tf_op jit(solution)/shard_map/reduce_scatter | solution.py:24
  142.6 60.8 %all-gather.51.cloned.1.call-start = ((), (), s32[]{:S(2)}) async-start(), calls=%async_computation.47 | async-start | bytes 2621440 | tf_op jit(solution)/shard_map/all_gather | solution.py:211
  143.4 75.3 %all-gather.49.cloned.1.call-start = ((), (), s32[]{:S(2)}) async-start(), calls=%async_computation.46 | async-start | bytes 6291456 | tf_op jit(solution)/shard_map/all_gather | solution.py:212
  144.2 105.9 %all-gather.27.cloned.1.call-start = ((), (), s32[]{:S(2)}) async-start(), calls=%async_computation.20 | async-start | bytes 1310720 | tf_op jit(solution)/shard_map/all_gather | solution.py:20
  171.1 93.4 %all-gather.53.cloned.1.call-start = ((), (), s32[]{:S(2)}) async-start(), calls=%async_computation.48 | async-start | bytes 6291456 | tf_op jit(solution)/shard_map/all_gather | solution.py:212
  203.5 94.4 %reduce-scatter.19.cloned.1.call-start = ((), (), s32[]{:S(2)}) async-start(), calls=%async_computation.21 | async-start | bytes 1310720 | tf_op jit(solution)/shard_map/reduce_scatter | solution.py:24
  269.3 57.1 %all-gather.29.cloned.1.call-start = ((), (), s32[]{:S(2)}) async-start(), calls=%async_computation.22 | async-start | bytes 1310720 | tf_op jit(solution)/shard_map/all_gather | solution.py:20
  299.7 68.0 %reduce-scatter.21.cloned.1.call-start = ((), (), s32[]{:S(2)}) async-start(), calls=%async_computation.23 | async-start | bytes 1310720 | tf_op jit(solution)/shard_map/reduce_scatter | solution.py:24
  370.8 57.9 %all-gather.33.cloned.1.call-start = ((), (), s32[]{:S(2)}) async-start(), calls=%async_computation.26 | async-start | bytes 1310720 | tf_op jit(solution)/shard_map/all_gather | solution.py:16
  371.6 91.3 %reduce-scatter.25.cloned.1.call-start = ((), (), s32[]{:S(2)}) async-start(), calls=%async_computation.27 | async-start | bytes 1310720 | tf_op jit(solution)/shard_map/reduce_scatter | solution.py:24
  442.0 78.4 %all-gather.35.cloned.1.call-start = ((), (), s32[]{:S(2)}) async-start(), calls=%async_computation.28 | async-start | bytes 1310720 | tf_op jit(solution)/shard_map/all_gather | solution.py:20
  493.7 65.3 %reduce-scatter.27.cloned.1.call-start = ((), (), s32[]{:S(2)}) async-start(), calls=%async_computation.29 | async-start | bytes 1310720 | tf_op jit(solution)/shard_map/reduce_scatter | solution.py:24
  562.3 61.9 %reduce-scatter.29.cloned.1.call-start = ((), (), s32[]{:S(2)}) async-start(), calls=%async_computation.31 | async-start | bytes 1310720 | tf_op jit(solution)/shard_map/reduce_scatter | solution.py:24
  597.3 57.3 %all-gather.39.cloned.1.call-start = ((), (), s32[]{:S(2)}) async-start(), calls=%async_computation.32 | async-start | bytes 1310720 | tf_op jit(solution)/shard_map/all_gather | solution.py:20
  628.0 68.4 %reduce-scatter.47.cloned.1.call-start = ((), (), s32[]{:S(2)}) async-start(), calls=%async_computation.41 | async-start | bytes 2621440 | tf_op jit(solution)/shard_map/reduce_scatter | solution.py:242
  632.9 97.3 %reduce-scatter.45.cloned.1.call-start = ((), (), s32[]{:S(2)}) async-start(), calls=%async_computation.40 | async-start | bytes 2621440 | tf_op jit(solution)/shard_map/reduce_scatter | solution.py:242
  638.4 130.1 %reduce-scatter.43.cloned.1.call-start = ((), (), s32[]{:S(2)}) async-start(), calls=%async_computation.39 | async-start | bytes 2621440 | tf_op jit(solution)/shard_map/reduce_scatter | solution.py:242
  642.6 163.8 %reduce-scatter.41.cloned.1.call-start = ((), (), s32[]{:S(2)}) async-start(), calls=%async_computation.38 | async-start | bytes 2621440 | tf_op jit(solution)/shard_map/reduce_scatter | solution.py:242
  646.9 189.6 %reduce-scatter.31.cloned.1.call-start = ((), (), s32[]{:S(2)}) async-start(), calls=%async_computation.33 | async-start | bytes 1310720 | tf_op jit(solution)/shard_map/reduce_scatter | solution.py:24
  666.9 196.6 %reduce-scatter.39.cloned.1.call-start = ((), (), s32[]{:S(2)}) async-start(), calls=%async_computation.37 | async-start | bytes 655360 | tf_op jit(solution)/shard_map/reduce_scatter | solution.py:242
  668.2 223.8 %reduce-scatter.37.cloned.1.call-start = ((), (), s32[]{:S(2)}) async-start(), calls=%async_computation.36 | async-start | bytes 655360 | tf_op jit(solution)/shard_map/reduce_scatter | solution.py:242
  670.9 255.2 %reduce-scatter.35.cloned.1.call-start = ((), (), s32[]{:S(2)}) async-start(), calls=%async_computation.35 | async-start | bytes 1966080 | tf_op jit(solution)/shard_map/reduce_scatter | solution.py:242
  678.7 281.5 %reduce-scatter.33.cloned.1.call-start = ((), (), s32[]{:S(2)}) async-start(), calls=%async_computation.34 | async-start | bytes 1966080 | tf_op jit(solution)/shard_map/reduce_scatter | solution.py:242
  732.2 75.5 %collective-permute-start.5 = (bf16[1024,256]{1,0:T(8,128)(2,1)}, bf16[1024,256]{1,0:T(8,128)(2,1)}, u32[]{:S(2)}, u32[]{:S(2)}) collective-permute-start(bf16[1024,256]{1,0:T(8,128)(2,1)} %broadcast_select_fusion), channel_id=1, source_target_pairs={{0,16},{16,0},{1,17},{17,1},{2,18},{18,2},{3,19},{19,3},{4,20},{20... | collective-permute-start | bytes 1572872 | tf_op jit(solution)/shard_map/ppermute | solution.py:156
  843.1 245.9 %all-reduce.3.cloned.1.call-start = ((), (), s32[]{:S(2)}) async-start(), calls=%async_computation.49 | async-start | bytes 196608
  893.0 68.4 %collective-permute-start.3 = (bf16[256,256]{1,0:T(8,128)(2,1)S(1)}, bf16[256,256]{1,0:T(8,128)(2,1)S(1)}, u32[]{:S(2)}, u32[]{:S(2)}) collective-permute-start(bf16[256,256]{1,0:T(8,128)(2,1)S(1)} %broadcast_select_fusion.3), channel_id=1, source_target_pairs={{0,16},{16,0},{1,17},{17,1},{2,18},{18,2},{3,19},{19,3},{4,20},{20... | collective-permute-start | bytes 393224 | tf_op jit(solution)/shard_map/ppermute | solution.py:156
  895.2 200.2 %collective-permute-start.1 = (bf16[512,256]{1,0:T(8,128)(2,1)S(1)}, bf16[512,256]{1,0:T(8,128)(2,1)S(1)}, u32[]{:S(2)}, u32[]{:S(2)}) collective-permute-start(bf16[512,256]{1,0:T(8,128)(2,1)S(1)} %get-tuple-element.55), channel_id=1, source_target_pairs={{0,16},{16,0},{1,17},{17,1},{2,18},{18,2},{3,19},{19,3},{4,20},{20... | collective-permute-start | bytes 786440 | tf_op jit(solution)/shard_map/ppermute | solution.py:156
  961.4 135.0 %collective-permute-start.2 = (bf16[256,4,192]{0,2,1:T(8,128)(2,1)S(1)}, bf16[256,4,192]{0,2,1:T(8,128)(2,1)S(1)}, u32[]{:S(2)}, u32[]{:S(2)}) collective-permute-start(bf16[256,4,192]{0,2,1:T(8,128)(2,1)S(1)} %broadcast_select_fusion.2), channel_id=1, source_target_pairs={{0,16},{16,0},{1,17},{17,1},{2,18},{18,2},{3,19},{19,3},{4,20},{20... | collective-permute-start | bytes 1179656 | tf_op jit(solution)/shard_map/ppermute | solution.py:156
  (67 other events, 2034.8 us)
Sparse Core Ops, SparseCore 0:
  9.8 33.4 all-gather.40
  45.4 29.9 all-gather.24
  77.0 10.4 all-gather.42
  88.9 10.1 all-gather.44
  100.9 36.4 all-gather.46
  142.8 25.2 reduce-scatter.16
  169.9 33.5 all-gather.50
  205.0 13.6 all-gather.48
  220.9 29.1 all-gather.26
  251.4 13.0 all-gather.52
  269.4 28.4 reduce-scatter.18
  299.9 26.4 all-gather.28
  341.1 26.6 reduce-scatter.20
  370.9 26.4 all-gather.30
  399.4 29.2 all-gather.32
  437.3 25.5 reduce-scatter.24
  465.6 25.7 reduce-scatter.22
  493.9 26.4 all-gather.34
  532.4 26.6 reduce-scatter.26
  562.4 26.4 all-gather.36
  597.4 26.6 reduce-scatter.28
  628.1 26.4 all-gather.38
  657.6 34.5 reduce-scatter.46
  695.0 35.1 reduce-scatter.44
  733.2 35.1 reduce-scatter.42
  771.3 35.1 reduce-scatter.40
  809.2 27.2 reduce-scatter.30
  839.9 23.5 reduce-scatter.38
  866.9 25.0 reduce-scatter.36
  894.9 31.1 reduce-scatter.34
  929.1 31.1 reduce-scatter.32
  966.4 122.6 all-reduce.2
